TPU v7x, 512 devices: a whole 4x4x16 slice. The times are simulated.
512 devices in a mesh: tile: 128 (over z, x, core), layer: 4 (over y).
Axes of the slice: x: 4, y: 4, z: 16, core: 2. Of those that a mesh axis runs over, the one named last changes fastest.
Arguments:
- head_start: float32 [8, 8192, 512], P('layer', 'tile'), may hold values from -2 to 0.5
- soil_class: int32 [8, 8192, 512], P('layer', 'tile'), may hold values from 0 to 11
- land_mask: int32 [8192, 512], P('tile'), may hold values 0 or 1
- ks_table: float32 [12], replicated, may hold values from 0.2 to 5
- alpha_table: float32 [12], replicated, may hold values from 0.5 to 2
- store_table: float32 [12], replicated, may hold values from 0.5 to 2
- section: float32 [2048, 128], P('tile'), may hold values from -6 to 6
- cross_owner: int32 [128, 256], P('tile'), may hold values from 0 to 127, as said below
- cross_local: int32 [128, 256], P('tile'), may hold values from 0 to 15
- node_cell: int32 [128, 256, 128], P('tile'), may hold values from -1 to 32767, as said below
- bed_cond: float32 [128, 256, 128], P('tile'), may hold values from 0.5 to 4
Outputs:
- head: float32 [8, 8192, 512], P('layer', 'tile')
- inflow: float32 [2048, 128], P('tile', 'layer')
Inputs may be any that keep to these rules, and one draw needn't show every extreme that they name: `cross_owner`: no strip's row names one owner in more than 2 slots, and in every row some owner is named in exactly 2 slots. `node_cell`: -1 marks a node outside the strip; other values index the strip's top-layer cells row-major over 64 x 512. In each strip the slots with nodes come first, the rest are padding with every node -1.
All inputs are finite; a program needn't handle non-finite values. No bound on the sum of `land_mask` on one device may be relied on, other than what follows from the above.
Results may differ from a plain program's by a relative error of at most 0.00002.
Values sent between devices are 32-bit elements; how exact they have to be, the bound alone decides.
A program may use at most 64 MiB of HBM per device.

v0:
```python
import jax
import jax.numpy as jnp
from jax import lax
from jax.sharding import PartitionSpec as P

ITERS = 2
SWEEPS = 3
LATERAL = 1.0
VERTICAL = 2.0
GRAVITY = 1.0
NEIGHBOURS = (
    (0, -1, VERTICAL),
    (0, 1, VERTICAL),
    (1, -1, LATERAL),
    (1, 1, LATERAL),
    (2, -1, LATERAL),
    (2, 1, LATERAL),
)


def with_halo(block, sides, width):
    for axis, dim in sides:
        count = lax.axis_size(axis)
        forward = [(i, i + 1) for i in range(count - 1)]
        backward = [(target, source) for source, target in forward]
        low = lax.ppermute(
            lax.slice_in_dim(block, block.shape[dim] - width, None, axis=dim), axis, forward
        )
        high = lax.ppermute(lax.slice_in_dim(block, 0, width, axis=dim), axis, backward)
        block = jnp.concatenate([low, block, high], axis=dim)
    return block


def from_root(value, axis, source):
    kept = jnp.where(lax.axis_index(axis) == source, value, 0).astype(value.dtype)
    return lax.psum(kept, axis)


def beside(padded, axis_id, step):
    spans = [slice(1, -1), slice(1, -1), slice(1, -1)]
    spans[axis_id] = slice(1 + step, padded.shape[axis_id] - 1 + step)
    return padded[tuple(spans)]


def neighbor_weights(cond_pad, open_pad):
    centre = cond_pad[1:-1, 1:-1, 1:-1]
    centre_open = open_pad[1:-1, 1:-1, 1:-1]
    result = []
    for axis_id, step, factor in NEIGHBOURS:
        far = beside(cond_pad, axis_id, step)
        far_open = beside(open_pad, axis_id, step)
        result.append(factor * 2.0 * centre_open * far_open / (centre + far))
    return result


def relax(head_pad, weights, store, head_old, riv_diag, riv_rhs):
    total = store * head_old
    diagonal_sum = store
    for weight, (axis_id, step, factor) in zip(weights, NEIGHBOURS):
        total = total + weight * beside(head_pad, axis_id, step)
        diagonal_sum = diagonal_sum + weight
    total = total + GRAVITY * (weights[0] - weights[1]) + riv_rhs
    return total / (diagonal_sum + riv_diag)


def lookup(values_table, classes):
    result = jnp.zeros(classes.shape, jnp.float32)
    for class_id in range(values_table.shape[0]):
        result = jnp.where(classes == class_id, values_table[class_id], result)
    return result


def pad_dims(field, chosen_dims):
    widths = [(1, 1) if place in chosen_dims else (0, 0) for place in range(field.ndim)]
    return jnp.pad(field, widths)


def pick_heads(top_head, cells):
    breadth = top_head.shape[1]
    slots, width = cells.shape
    group = 16
    grouped = cells.reshape(slots // group, group * width)
    columns = jnp.arange(breadth, dtype=jnp.int32)[None, :]

    def one_group(flat_cells):
        picked_rows = jnp.take(top_head, flat_cells // breadth, axis=0)
        hit = columns == (flat_cells % breadth)[:, None]
        return jnp.sum(jnp.where(hit, picked_rows, 0.0), axis=1)

    return lax.map(one_group, grouped).reshape(slots, width)


def on_device(
    head_start,
    soil_class,
    land_mask,
    ks_table,
    alpha_table,
    store_table,
    section,
    cross_owner,
    cross_local,
    node_cell,
    bed_cond,
):
    layers, across, breadth = head_start.shape
    reach_rows = section.shape[0]
    node_count = section.shape[1]
    tile_count = lax.axis_size("tile")
    quarter = node_count // lax.axis_size("layer")
    node_first = lax.axis_index("layer") * quarter
    ks = lookup(ks_table, soil_class)
    alpha = lookup(alpha_table, soil_class)
    store = lookup(store_table, soil_class)
    landf = land_mask.astype(jnp.float32)[None]
    owners = cross_owner[0]
    positions = cross_local[0]
    node_cells = node_cell[0]
    bed_given = bed_cond[0]
    whole_section = lax.all_gather(section, "tile", axis=0, tiled=True)
    slot_section = jnp.take(whole_section, owners * reach_rows + positions, axis=0)
    in_tile = node_cells >= 0
    flat_index = jnp.where(in_tile, node_cells, across * breadth)
    bed_terms = jnp.where(in_tile, bed_given, 0.0)
    diag_top = (
        jnp.zeros((across * breadth,), jnp.float32)
        .at[flat_index.reshape(-1)]
        .add(bed_terms.reshape(-1), mode="drop")
    )
    rhs_top = (
        jnp.zeros((across * breadth,), jnp.float32)
        .at[flat_index.reshape(-1)]
        .add((bed_terms * slot_section).reshape(-1), mode="drop")
    )
    top_diag = diag_top.reshape(across, breadth)
    top_rhs = rhs_top.reshape(across, breadth)
    head_old, ks_here, alpha_here, store_here, land_here = (head_start, ks, alpha, store, landf)
    on_top = (lax.axis_index("layer") == 0).astype(jnp.float32)
    riv_diag = jnp.zeros((layers, across, breadth), jnp.float32).at[0].set(top_diag * on_top)
    riv_rhs = jnp.zeros((layers, across, breadth), jnp.float32).at[0].set(top_rhs * on_top)

    def head_halo(field):
        return pad_dims(with_halo(field, (("tile", 1), ("layer", 0)), 1), (2,))

    head = head_old
    for picard in range(ITERS):
        head_pad = head_halo(head)
        conduct = ks_here * jnp.exp(alpha_here * jnp.minimum(head, 0.0))
        both_pad = pad_dims(
            with_halo(jnp.stack([conduct, conduct * land_here]), (("tile", 2), ("layer", 1)), 1),
            (3,),
        )
        cond_pad = both_pad[0]
        open_pad = both_pad[1]
        weights = neighbor_weights(cond_pad, open_pad)
        for sweep in range(SWEEPS):
            if sweep > 0:
                head_pad = head_halo(head)
            head = relax(head_pad, weights, store_here, head_old, riv_diag, riv_rhs)
    top_head = from_root(head[0], "layer", 0)
    my_cells = lax.dynamic_slice_in_dim(node_cells, node_first, quarter, 1)
    my_bed = lax.dynamic_slice_in_dim(bed_given, node_first, quarter, 1)
    my_section = lax.dynamic_slice_in_dim(slot_section, node_first, quarter, 1)
    my_inside = my_cells >= 0
    node_head = pick_heads(top_head, jnp.where(my_inside, my_cells, 0))
    slot_in = jnp.where(my_inside, my_bed * (node_head - my_section), 0.0)
    dense = (
        jnp.zeros((reach_rows * tile_count, quarter), jnp.float32)
        .at[owners * reach_rows + positions]
        .add(slot_in)
    )
    inflow = lax.psum_scatter(dense, "tile", scatter_dimension=0, tiled=True)
    return (head, inflow)


def solution(mesh):
    placed = (
        P("layer", "tile", None),
        P("layer", "tile", None),
        P("tile", None),
        P(),
        P(),
        P(),
        P("tile", None),
        P("tile", None),
        P("tile", None),
        P("tile", None, None),
        P("tile", None, None),
    )
    return jax.shard_map(
        on_device,
        mesh=mesh,
        in_specs=placed,
        out_specs=(P("layer", "tile", None), P("tile", "layer")),
        check_vma=False,
    )
```

profile of v0, /device:TPU:8, one launch (start us, length us, event | category | flops | bytes accessed | tf_op | source)
XLA Modules:
  0.0 1032.4 jit_solution(11896485293692213495)
XLA Ops:
  11.7 17.8 %fusion.107 = (f32[1,2,64,512]{3,2,1,0:T(8,128)S(1)}, f32[2,64,512]{2,1,0:T(8,128)S(1)}, f32[2,64,512]{2,1,0:T(8,128)S(1)}, pred[2,64,512]{2,1,0:T(8,128)(4,1)S(...) fusion(f32[2,64,512]{2,1,0:T(8,128)} %param.17, ...), kind=kLoop, calls=%fused_computation.316 | loop fusion | flops 2555904 | bytes 2097248 | tf_op jit(solution)/shard_map/stack | solution.py:150
  31.0 3.0 collective-permute-start
  35.3 3.6 collective-permute-start.4
  40.6 7.1 collective-permute-start.7
  49.8 3.9 collective-permute-start.3
  56.7 4.8 collective-permute-done.3
  61.5 3.4 collective-permute-done.2
  66.5 8.5 add_add_fusion.1
  76.1 104.6 %all-gather.2.cloned.1.call-done = f32[2048,128]{1,0:T(8,128)} async-done(((f32[16,128]{1,0:T(8,128)}), f32[2048,128]{1,0:T(8,128)}) %all-gather.2.cloned.1.call-update) | async-done | bytes 1048592 | tf_op jit(solution)/shard_map/all_gather | solution.py:120
  184.3 171.3 %scatter_custom_fusion.1 = f32[32768]{0:T(1024)S(1)} fusion(s32[32768]{0:T(1024)} %bitcast.101, f32[32768]{0:T(1024)S(1)} %get-tuple-element.136, f32[]{:T(128)} %constant.189.clone.1), kind=kCustom, calls=%fused_computation.302 | custom fusion | flops 32768 | bytes 131584 | tf_op jit(solution)/shard_map/scatter-add | solution.py:128
  357.3 171.2 %scatter_custom_fusion = f32[32768]{0:T(1024)S(1)} fusion(s32[32768]{0:T(1024)} %bitcast.102, f32[32768]{0:T(1024)} %get-tuple-element.134, f32[]{:T(128)} %constant.189.clone.1), kind=kCustom, calls=%fused_computation.304 | custom fusion | flops 32768 | bytes 131584 | tf_op jit(solution)/shard_map/scatter-add | solution.py:133
  534.0 3.0 collective-permute-start.8
  537.9 2.4 collective-permute-start.11
  540.3 3.4 collective-permute-start.10
  543.7 2.4 collective-permute-done.11
  546.1 2.7 collective-permute-done.10
  550.9 3.0 collective-permute-start.12
  556.7 3.9 collective-permute-start.14
  560.6 2.0 collective-permute-done.15
  567.5 3.1 collective-permute-start.20
  572.0 5.1 collective-permute-start.16
  580.0 3.9 collective-permute-start.18
  585.9 4.1 collective-permute-start.22
  590.0 2.6 collective-permute-done.23
  598.7 3.0 collective-permute-start.24
  604.6 3.9 collective-permute-start.26
  613.7 4.8 collective-permute-start.28
  621.9 3.9 collective-permute-start.30
  630.5 75.9 %all-reduce.10.cloned.1.call-done = f32[64,512]{1,0:T(8,128)} async-done(((f32[64,512]{1,0:T(8,128)}), f32[64,512]{1,0:T(8,128)}) %all-reduce.10.cloned.1.call-update) | async-done | bytes 131088 | tf_op jit(solution)/shard_map/psum | solution.py:36
  706.4 54.5 %while.15 = (s32[]{:T(128)}, f32[16,512]{1,0:T(8,128)S(1)}, s32[16,512]{1,0:T(8,128)S(1)}, f32[64,512]{1,0:T(8,128)}, s32[]{:T(128)}, /*index=5*/s32[]{:T(128)}) while((s32[]{:T(128)}, f32[16,512]{1,0:T(8,128)S(1)}, s32[16,512]{1,0:T(8,128)S(1)}, f32[64,512]{1,0:T(8,128)}, s32[]{:T(128)}, /*index=5*/s32[]{:T(128)}) %tuple.130), condition=%wide.region_5.6_spmd.clone, body=%wide.region_3.5_spmd.clone.sunk | while | flops 1074690 | bytes 3175509 | solution.py:90
  706.4 3.0 gather_fusion
  709.9 2.9 gather_fusion
  713.3 2.9 gather_fusion
  716.7 2.9 gather_fusion
  720.1 2.9 gather_fusion
  723.5 2.9 gather_fusion
  726.9 2.9 gather_fusion
  730.3 2.9 gather_fusion
  733.7 2.9 gather_fusion
  737.1 2.9 gather_fusion
  740.5 2.9 gather_fusion
  743.9 2.9 gather_fusion
  747.3 2.9 gather_fusion
  750.7 2.9 gather_fusion
  754.1 2.9 gather_fusion
  757.5 2.9 gather_fusion
  761.0 2.6 scatter_custom_fusion.2
  763.6 262.3 %reduce-scatter.2.cloned.1.call-done = f32[16,32]{1,0:T(8,128)} async-done(((f32[2048,32]{1,0:T(8,128)}), f32[16,32]{1,0:T(8,128)}) %reduce-scatter.2.cloned.1.call-update) | async-done | bytes 2064 | tf_op jit(solution)/shard_map/reduce_scatter | solution.py:172
  (267 shorter events, 72.3 us)
Async XLA Ops:
  7.2 22.4 %copy-start = (f32[2,64,512]{2,1,0:T(8,128)S(1)}, f32[2,64,512]{2,1,0:T(8,128)}, u32[]{:S(2)}) copy-start(f32[2,64,512]{2,1,0:T(8,128)} %param.17) | copy-start | bytes 786436
  7.2 173.5 %all-gather.2.cloned.1.call-start = ((), (), s32[]{:S(2)}) async-start(), calls=%async_computation.1 | async-start | bytes 1056768 | tf_op jit(solution)/shard_map/all_gather | solution.py:120
  11.7 17.9 %copy-start.2 = (f32[64,512]{1,0:T(8,128)}, f32[64,512]{1,0:T(8,128)S(1)}, u32[]{:S(2)}) copy-start(f32[64,512]{1,0:T(8,128)S(1)} %convert_element_type.18) | copy-start | bytes 393220
  11.7 27.3 %copy-start.1 = (s32[1,256,128]{2,1,0:T(8,128)S(1)}, s32[1,256,128]{2,1,0:T(8,128)}, u32[]{:S(2)}) copy-start(s32[1,256,128]{2,1,0:T(8,128)} %param.26) | copy-start | bytes 393220
  29.6 10.4 %copy-start.22 = (s32[1,256]{1,0:T(1,128)S(1)}, s32[1,256]{1,0:T(1,128)}, u32[]{:S(2)}) copy-start(s32[1,256]{1,0:T(1,128)} %param.25) | copy-start | bytes 3076
  29.6 10.4 %copy-start.23 = (s32[1,256]{1,0:T(1,128)S(1)}, s32[1,256]{1,0:T(1,128)}, u32[]{:S(2)}) copy-start(s32[1,256]{1,0:T(1,128)} %param.24) | copy-start | bytes 3076
  29.7 19.9 %collective-permute-start.1 = (f32[2,2,1,512]{3,2,1,0:T(1,128)S(1)}, f32[2,2,1,512]{3,2,1,0:T(1,128)S(1)}, u32[]{:S(2)}, u32[]{:S(2)}) collective-permute-start(f32[2,2,1,512]{3,2,1,0:T(1,128)S(1)} %get-tuple-element.168), channel_id=1, source_target_pairs={{4,0},{8,4},{12,8},{16,12},{20,16},{24,20},{28,24},{32,28},{36,32}... | collective-permute-start | bytes 24584 | tf_op jit(solution)/shard_map/ppermute | solution.py:29
  31.0 18.6 %collective-permute-start = (f32[2,2,1,512]{3,2,1,0:T(1,128)S(1)}, f32[2,2,1,512]{3,2,1,0:T(1,128)S(1)}, u32[]{:S(2)}, u32[]{:S(2)}) collective-permute-start(f32[2,2,1,512]{3,2,1,0:T(1,128)S(1)} %get-tuple-element.167), channel_id=1, source_target_pairs={{0,4},{4,8},{8,12},{12,16},{16,20},{20,24},{24,28},{28,32},{32,36}... | collective-permute-start | bytes 24584 | tf_op jit(solution)/shard_map/ppermute | solution.py:26
  34.0 6.4 collective-permute-start.5
  35.3 5.1 collective-permute-start.4
  39.0 667.3 %all-reduce.10.cloned.1.call-start = ((), (), s32[]{:S(2)}) async-start(), calls=%async_computation.2 | async-start | bytes 262144 | tf_op jit(solution)/shard_map/psum | solution.py:36
  40.5 15.1 %copy-start.21 = (f32[12]{0:T(128)S(1)}, f32[12]{0:T(128)}, u32[]{:S(2)}) copy-start(f32[12]{0:T(128)} %param.22) | copy-start | bytes 148
  40.6 15.8 %collective-permute-start.7 = (f32[1,66,512]{2,1,0:T(8,128)S(1)}, f32[1,66,512]{2,1,0:T(8,128)S(1)}, u32[]{:S(2)}, u32[]{:S(2)}) collective-permute-start(f32[1,66,512]{2,1,0:T(8,128)S(1)} %get-tuple-element.180), channel_id=1, source_target_pairs={{1,0},{2,1},{3,2},{5,4},{6,5},{7,6},{9,8},{10,9},{11,10},{13,12},{... | collective-permute-start | bytes 405512 | tf_op jit(solution)/shard_map/ppermute | solution.py:29
  47.7 8.7 collective-permute-start.6
  49.8 11.8 %collective-permute-start.3 = (f32[2,1,66,512]{3,2,1,0:T(8,128)S(1)}, f32[2,1,66,512]{3,2,1,0:T(8,128)S(1)}, u32[]{:S(2)}, u32[]{:S(2)}) collective-permute-start(f32[2,1,66,512]{3,2,1,0:T(8,128)S(1)} %get-tuple-element.164), channel_id=1, source_target_pairs={{1,0},{2,1},{3,2},{5,4},{6,5},{7,6},{9,8},{10,9},{11,10},{13,12},{... | collective-permute-start | bytes 811016 | tf_op jit(solution)/shard_map/ppermute | solution.py:29
  53.7 11.2 %collective-permute-start.2 = (f32[2,1,66,512]{3,2,1,0:T(8,128)S(1)}, f32[2,1,66,512]{3,2,1,0:T(8,128)S(1)}, u32[]{:S(2)}, u32[]{:S(2)}) collective-permute-start(f32[2,1,66,512]{3,2,1,0:T(8,128)S(1)} %get-tuple-element.163), channel_id=1, source_target_pairs={{0,1},{1,2},{2,3},{4,5},{5,6},{6,7},{8,9},{9,10},{10,11},{12,13},{... | collective-permute-start | bytes 811016 | tf_op jit(solution)/shard_map/ppermute | solution.py:26
  56.4 9.1 copy-start.6
  56.4 9.0 copy-start.8
  66.5 8.5 copy-start.9
  357.3 180.6 %copy-start.4 = (f32[1,64,512]{2,1,0:T(8,128)}, f32[1,64,512]{2,1,0:T(8,128)S(1)}, u32[]{:S(2)}) copy-start(f32[1,64,512]{2,1,0:T(8,128)S(1)} %mul.274) | copy-start | bytes 393220
  532.7 4.3 collective-permute-start.9
  534.0 3.8 collective-permute-start.8
  537.9 8.2 collective-permute-start.11
  540.3 8.4 collective-permute-start.10
  549.5 4.3 collective-permute-start.13
  550.9 3.8 collective-permute-start.12
  554.8 7.9 collective-permute-start.15
  556.7 7.9 collective-permute-start.14
  566.2 10.9 %collective-permute-start.21 = (f32[2,1,512]{2,1,0:T(1,128)S(1)}, f32[2,1,512]{2,1,0:T(1,128)S(1)}, u32[]{:S(2)}, u32[]{:S(2)}) collective-permute-start(f32[2,1,512]{2,1,0:T(1,128)S(1)} %get-tuple-element.186), channel_id=1, source_target_pairs={{4,0},{8,4},{12,8},{16,12},{20,16},{24,20},{28,24},{32,28},{36,32}... | collective-permute-start | bytes 12296 | tf_op jit(solution)/shard_map/ppermute | solution.py:29
  567.5 9.6 collective-permute-start.20
  570.7 6.5 collective-permute-start.17
  572.0 6.0 collective-permute-start.16
  578.0 16.8 %collective-permute-start.19 = (f32[2,1,66,512]{3,2,1,0:T(8,128)S(1)}, f32[2,1,66,512]{3,2,1,0:T(8,128)S(1)}, u32[]{:S(2)}, u32[]{:S(2)}) collective-permute-start(f32[2,1,66,512]{3,2,1,0:T(8,128)S(1)} %get-tuple-element.162), channel_id=1, source_target_pairs={{1,0},{2,1},{3,2},{5,4},{6,5},{7,6},{9,8},{10,9},{11,10},{13,12},{... | collective-permute-start | bytes 811016 | tf_op jit(solution)/shard_map/ppermute | solution.py:29
  580.0 14.9 %collective-permute-start.18 = (f32[2,1,66,512]{3,2,1,0:T(8,128)S(1)}, f32[2,1,66,512]{3,2,1,0:T(8,128)S(1)}, u32[]{:S(2)}, u32[]{:S(2)}) collective-permute-start(f32[2,1,66,512]{3,2,1,0:T(8,128)S(1)} %get-tuple-element.161), channel_id=1, source_target_pairs={{0,1},{1,2},{2,3},{4,5},{5,6},{6,7},{8,9},{9,10},{10,11},{12,13},{... | collective-permute-start | bytes 811016 | tf_op jit(solution)/shard_map/ppermute | solution.py:26
  583.9 8.7 collective-permute-start.23
  585.9 8.7 collective-permute-start.22
  597.4 4.3 collective-permute-start.25
  598.7 3.8 collective-permute-start.24
  602.6 7.0 collective-permute-start.27
  604.6 7.0 collective-permute-start.26
  612.4 6.1 collective-permute-start.29
  613.7 5.6 collective-permute-start.28
  620.0 7.2 collective-permute-start.31
  621.9 7.0 collective-permute-start.30
  629.7 76.7 %copy-start.10 = (f32[2,64,512]{2,1,0:T(8,128)}, f32[2,64,512]{2,1,0:T(8,128)S(1)}, u32[]{:S(2)}) copy-start(f32[2,64,512]{2,1,0:T(8,128)S(1)} %div.91) | copy-start | bytes 786436
  630.4 395.5 %reduce-scatter.2.cloned.1.call-start = ((), (), s32[]{:S(2)}) async-start(), calls=%async_computation.3 | async-start | bytes 1056768 | tf_op jit(solution)/shard_map/reduce_scatter | solution.py:172
  706.4 54.6 %copy-start.11 = (f32[1,256,128]{2,1,0:T(8,128)S(1)}, f32[1,256,128]{2,1,0:T(8,128)}, u32[]{:S(2)}) copy-start(f32[1,256,128]{2,1,0:T(8,128)} %param.27) | copy-start | bytes 393220
  706.4 54.6 %copy-start.12 = (f32[256,128]{1,0:T(8,128)S(1)}, f32[256,128]{1,0:T(8,128)}, u32[]{:S(2)}) copy-start(f32[256,128]{1,0:T(8,128)} %get-tuple-element.135) | copy-start | bytes 393220
  (11 other events, 17.7 us)
Sparse Core Ops, SparseCore 0:
  39.1 141.4 all-gather.1
  630.6 75.7 all-reduce.9
  763.7 262.1 reduce-scatter.1
where the time goes:
time: 1030 us
  waiting for transfers between devices  475 us (46%)
  other arithmetic  393 us (38%)
  starting transfers between devices  89.4 us (9%)
  local copies, waits for them, and re-layouts  59.6 us (6%)
  between operations  14.7 us (1%)
    reduce_scatter x1, waiting for transfers between devices, on_device(): inflow = lax.psum_scatter(dense, 'tile', scatter_dimension=0, tiled=True)  262 us
    scatter-add x1, other arithmetic, on_device(): diag_top = jnp.zeros((across * breadth,), jnp.float32).at[flat_index.resh...  171 us
    scatter-add x1, other arithmetic, on_device(): rhs_top = jnp.zeros((across * breadth,), jnp.float32).at[flat_index.resha...  171 us
    all_gather x1, waiting for transfers between devices, on_device(): whole_section = lax.all_gather(section, 'tile', axis=0, tiled=True)  105 us
    psum x1, waiting for transfers between devices, from_root(): return lax.psum(kept, axis)  75.9 us
    ppermute x16, starting transfers between devices, with_halo(): lax.ppermute(lax.slice_in_dim(block, block.shape[dim] - width, None, axis...  55.8 us
    gather x16, local copies, waits for them, and re-layouts, one_group(): picked_rows = jnp.take(top_head, flat_cells // breadth, axis=0)  47 us
    ppermute x16, starting transfers between devices, with_halo(): lax.ppermute(lax.slice_in_dim(block, 0, width, axis=dim), axis, backward)  33.4 us
  transfers between devices with their start and end apart: 35, of which 20 were waited for; matrix products, arithmetic and copies ran while one was open for 1% of the time, Pallas kernels for 0%

commit v1 on v0

--- a/solution.py
+++ b/solution.py
@@ -117,7 +117,10 @@
     positions = cross_local[0]
     node_cells = node_cell[0]
     bed_given = bed_cond[0]
-    whole_section = lax.all_gather(section, "tile", axis=0, tiled=True)
+    size = lax.axis_size("tile")
+    blocks = jnp.stack([section for _ in range(size)])
+    blocks = lax.all_to_all(blocks, "tile", split_axis=0, concat_axis=0)
+    whole_section = jnp.concatenate(blocks, axis=0)
     slot_section = jnp.take(whole_section, owners * reach_rows + positions, axis=0)
     in_tile = node_cells >= 0
     flat_index = jnp.where(in_tile, node_cells, across * breadth)

time: 1030 us -> 966 us (0.938)
  waiting for transfers between devices: 475 us -> 391 us
  starting transfers between devices: 89.4 us -> 107 us
    all_gather x1 -> x0, waiting for transfers between devices: 105 us -> none  [on_device(): whole_section = lax.all_gather(section, 'tile', axis=0, tiled=True)]
    all_to_all x0 -> x1, starting transfers between devices: none -> 26.5 us  [on_device(): blocks = lax.all_to_all(blocks, 'tile', split_axis=0, concat_axis=0)]
    all_to_all x0 -> x1, waiting for transfers between devices: none -> 19.9 us  [on_device(): blocks = lax.all_to_all(blocks, 'tile', split_axis=0, concat_axis=0)]
    ppermute x16, waiting for transfers between devices: 14.3 us -> 31.9 us  [with_halo(): lax.ppermute(lax.slice_in_dim(block, 0, width, axis=dim), axis, backward)]
    ppermute x16, starting transfers between devices: 55.8 us -> 44.7 us  [with_halo(): lax.ppermute(lax.slice_in_dim(block, block.shape[dim] - width, None, axis...]
  transfers between devices with their start and end apart: 35 -> 35, of which waited for: 20 -> 20; matrix products, arithmetic and copies ran while one was open for 1% -> 2% of each run, Pallas kernels for 0% -> 0%
where the time goes in v1:
time: 966 us; the launch traced here: 965 us
  waiting for transfers between devices  391 us (40%)
  other arithmetic  389 us (40%)
  starting transfers between devices  107 us (11%)
  local copies, waits for them, and re-layouts  60.7 us (6%)
  between operations  15.2 us (2%)
    reduce_scatter x1, waiting for transfers between devices, on_device(): inflow = lax.psum_scatter(dense, 'tile', scatter_dimension=0, tiled=True)  262 us
    scatter-add x1, other arithmetic, on_device(): diag_top = jnp.zeros((across * breadth,), jnp.float32).at[flat_index.resh...  171 us
    scatter-add x1, other arithmetic, on_device(): rhs_top = jnp.zeros((across * breadth,), jnp.float32).at[flat_index.resha...  171 us
    psum x1, waiting for transfers between devices, from_root(): return lax.psum(kept, axis)  66.4 us
    gather x16, local copies, waits for them, and re-layouts, one_group(): picked_rows = jnp.take(top_head, flat_cells // breadth, axis=0)  47 us
    ppermute x16, starting transfers between devices, with_halo(): lax.ppermute(lax.slice_in_dim(block, block.shape[dim] - width, None, axis...  44.7 us
    ppermute x16, starting transfers between devices, with_halo(): lax.ppermute(lax.slice_in_dim(block, 0, width, axis=dim), axis, backward)  36.1 us
    ppermute x16, waiting for transfers between devices, with_halo(): lax.ppermute(lax.slice_in_dim(block, 0, width, axis=dim), axis, backward)  31.9 us
  transfers between devices with their start and end apart: 35, of which 20 were waited for; matrix products, arithmetic and copies ran while one was open for 2% of the time, Pallas kernels for 0%

profile of v1, /device:TPU:8, one launch (start us, length us, event | category | flops | bytes accessed | tf_op | source)
XLA Modules:
  0.0 964.5 jit_solution(10779992966647085774)
XLA Ops:
  11.7 17.3 %fusion.107 = (f32[1,2,64,512]{3,2,1,0:T(8,128)S(1)}, f32[2,64,512]{2,1,0:T(8,128)S(1)}, f32[2,64,512]{2,1,0:T(8,128)S(1)}, pred[2,64,512]{2,1,0:T(8,128)(4,1)},...) fusion(f32[2,64,512]{2,1,0:T(8,128)} %param.17, ...), kind=kLoop, calls=%fused_computation.316 | loop fusion | flops 2555904 | bytes 2097248 | tf_op jit(solution)/shard_map/stack | solution.py:153
  32.9 4.3 collective-permute-start.4
  39.7 26.5 %all-to-all-start = ((f32[128,16,128]{2,1,0:T(8,128)}), f32[128,16,128]{2,1,0:T(8,128)S(1)}, u32[]{:S(2)}, u32[]{:S(2)}) async-start(f32[128,16,128]{2,1,0:T(8,128)} %stack.17), calls=%async_computation | async-start | bytes 2097152 | tf_op jit(solution)/shard_map/all_to_all | solution.py:122
  68.4 3.5 collective-permute-start.6
  74.4 3.5 collective-permute-start.2
  81.3 2.9 collective-permute-done.2
  84.3 3.2 collective-permute-done.3
  89.2 8.6 add_add_fusion.1
  99.7 19.9 %all-to-all-done = f32[128,16,128]{2,1,0:T(8,128)S(1)} async-done(((f32[128,16,128]{2,1,0:T(8,128)}), f32[128,16,128]{2,1,0:T(8,128)S(1)}, u32[]{:S(2)}, u32[]{:S(2)}) %all-to-all-start) | async-done | bytes 1048608 | tf_op jit(solution)/shard_map/all_to_all | solution.py:122
  122.0 171.3 %scatter_custom_fusion = f32[32768]{0:T(1024)S(1)} fusion(s32[32768]{0:T(1024)} %bitcast.103, f32[32768]{0:T(1024)S(1)} %get-tuple-element.134, f32[]{:T(128)} %constant.189.clone.1), kind=kCustom, calls=%fused_computation.304 | custom fusion | flops 32768 | bytes 131584 | tf_op jit(solution)/shard_map/scatter-add | solution.py:136
  293.4 171.3 %scatter_custom_fusion.1 = f32[32768]{0:T(1024)S(1)} fusion(s32[32768]{0:T(1024)} %bitcast.104, f32[32768]{0:T(1024)S(1)} %get-tuple-element.136, f32[]{:T(128)} %constant.189.clone.1), kind=kCustom, calls=%fused_computation.302 | custom fusion | flops 32768 | bytes 131584 | tf_op jit(solution)/shard_map/scatter-add | solution.py:131
  469.9 3.5 collective-permute-start.10
  476.9 3.6 collective-permute-done.11
  481.3 3.2 collective-permute-start.12
  485.8 3.4 collective-permute-done.13
  489.2 3.2 collective-permute-start.14
  492.4 2.8 collective-permute-start.15
  496.4 3.5 collective-permute-done.15
  501.6 2.9 collective-permute-start.20
  505.8 4.6 collective-permute-start.16
  511.8 2.9 collective-permute-done.17
  516.8 3.9 collective-permute-start.19
  522.7 3.9 collective-permute-start.23
  526.7 2.7 collective-permute-done.22
  538.5 3.6 collective-permute-done.25
  544.1 3.9 collective-permute-start.27
  552.0 3.2 collective-permute-start.28
  556.5 4.0 collective-permute-done.29
  563.1 3.9 collective-permute-start.31
  571.8 66.4 %all-reduce.10.cloned.1.call-done = f32[64,512]{1,0:T(8,128)} async-done(((f32[64,512]{1,0:T(8,128)}), f32[64,512]{1,0:T(8,128)}) %all-reduce.10.cloned.1.call-update) | async-done | bytes 131088 | tf_op jit(solution)/shard_map/psum | solution.py:36
  638.2 54.5 %while.15 = (s32[]{:T(128)}, f32[16,512]{1,0:T(8,128)S(1)}, s32[16,512]{1,0:T(8,128)S(1)}, f32[64,512]{1,0:T(8,128)}, s32[]{:T(128)}, /*index=5*/s32[]{:T(128)}) while((s32[]{:T(128)}, f32[16,512]{1,0:T(8,128)S(1)}, s32[16,512]{1,0:T(8,128)S(1)}, f32[64,512]{1,0:T(8,128)}, s32[]{:T(128)}, /*index=5*/s32[]{:T(128)}) %tuple.130), condition=%wide.region_5.6_spmd.clone, body=%wide.region_3.5_spmd.clone.sunk | while | flops 1074690 | bytes 3175501 | solution.py:90
  638.2 3.0 gather_fusion
  641.7 2.9 gather_fusion
  645.1 2.9 gather_fusion
  648.5 2.9 gather_fusion
  651.9 2.9 gather_fusion
  655.3 2.9 gather_fusion
  658.7 2.9 gather_fusion
  662.1 2.9 gather_fusion
  665.5 2.9 gather_fusion
  668.9 2.9 gather_fusion
  672.3 2.9 gather_fusion
  675.7 2.9 gather_fusion
  679.1 2.9 gather_fusion
  682.5 2.9 gather_fusion
  685.9 2.9 gather_fusion
  689.3 2.9 gather_fusion
  695.4 262.3 %reduce-scatter.2.cloned.1.call-done = f32[16,32]{1,0:T(8,128)} async-done(((f32[2048,32]{1,0:T(8,128)}), f32[16,32]{1,0:T(8,128)}) %reduce-scatter.2.cloned.1.call-update) | async-done | bytes 2064 | tf_op jit(solution)/shard_map/reduce_scatter | solution.py:175
  (293 shorter events, 77.7 us)
Async XLA Ops:
  7.2 22.5 %copy-start = (f32[2,64,512]{2,1,0:T(8,128)S(1)}, f32[2,64,512]{2,1,0:T(8,128)}, u32[]{:S(2)}) copy-start(f32[2,64,512]{2,1,0:T(8,128)} %param.17) | copy-start | bytes 786436
  11.7 18.1 %copy-start.10 = (f32[64,512]{1,0:T(8,128)}, f32[64,512]{1,0:T(8,128)S(1)}, u32[]{:S(2)}) copy-start(f32[64,512]{1,0:T(8,128)S(1)} %convert_element_type.18) | copy-start | bytes 393220
  11.7 27.0 %copy-start.34 = (f32[16,128]{1,0:T(8,128)S(1)}, f32[16,128]{1,0:T(8,128)}, u32[]{:S(2)}) copy-start(f32[16,128]{1,0:T(8,128)} %param.23) | copy-start | bytes 24580
  29.8 44.4 %collective-permute-start = (f32[2,2,1,512]{3,2,1,0:T(1,128)S(1)}, f32[2,2,1,512]{3,2,1,0:T(1,128)S(1)}, u32[]{:S(2)}, u32[]{:S(2)}) collective-permute-start(f32[2,2,1,512]{3,2,1,0:T(1,128)S(1)} %get-tuple-element.167), channel_id=1, source_target_pairs={{0,4},{4,8},{8,12},{12,16},{16,20},{20,24},{24,28},{28,32},{32,36}... | collective-permute-start | bytes 24584 | tf_op jit(solution)/shard_map/ppermute | solution.py:26
  31.6 42.7 %collective-permute-start.1 = (f32[2,2,1,512]{3,2,1,0:T(1,128)S(1)}, f32[2,2,1,512]{3,2,1,0:T(1,128)S(1)}, u32[]{:S(2)}, u32[]{:S(2)}) collective-permute-start(f32[2,2,1,512]{3,2,1,0:T(1,128)S(1)} %get-tuple-element.168), channel_id=1, source_target_pairs={{4,0},{8,4},{12,8},{16,12},{20,16},{24,20},{28,24},{32,28},{36,32}... | collective-permute-start | bytes 24584 | tf_op jit(solution)/shard_map/ppermute | solution.py:29
  32.9 34.7 %collective-permute-start.4 = (f32[2,1,512]{2,1,0:T(1,128)S(1)}, f32[2,1,512]{2,1,0:T(1,128)S(1)}, u32[]{:S(2)}, u32[]{:S(2)}) collective-permute-start(f32[2,1,512]{2,1,0:T(1,128)S(1)} %get-tuple-element.191), channel_id=1, source_target_pairs={{0,4},{4,8},{8,12},{12,16},{16,20},{20,24},{24,28},{28,32},{32,36}... | collective-permute-start | bytes 12296 | tf_op jit(solution)/shard_map/ppermute | solution.py:26
  37.2 29.0 %copy-start.8 = (s32[1,256,128]{2,1,0:T(8,128)S(1)}, s32[1,256,128]{2,1,0:T(8,128)}, u32[]{:S(2)}) copy-start(s32[1,256,128]{2,1,0:T(8,128)} %param.26) | copy-start | bytes 393220
  37.2 29.9 %copy-start.35 = (s32[1,256]{1,0:T(1,128)S(1)}, s32[1,256]{1,0:T(1,128)}, u32[]{:S(2)}) copy-start(s32[1,256]{1,0:T(1,128)} %param.25) | copy-start | bytes 3076
  37.2 29.9 %copy-start.36 = (s32[1,256]{1,0:T(1,128)S(1)}, s32[1,256]{1,0:T(1,128)}, u32[]{:S(2)}) copy-start(s32[1,256]{1,0:T(1,128)} %param.24) | copy-start | bytes 3076
  37.2 30.4 %collective-permute-start.5 = (f32[2,1,512]{2,1,0:T(1,128)S(1)}, f32[2,1,512]{2,1,0:T(1,128)S(1)}, u32[]{:S(2)}, u32[]{:S(2)}) collective-permute-start(f32[2,1,512]{2,1,0:T(1,128)S(1)} %get-tuple-element.192), channel_id=1, source_target_pairs={{4,0},{8,4},{12,8},{16,12},{20,16},{24,20},{28,24},{32,28},{36,32}... | collective-permute-start | bytes 12296 | tf_op jit(solution)/shard_map/ppermute | solution.py:29
  39.7 79.9 %all-to-all-start = ((f32[128,16,128]{2,1,0:T(8,128)}), f32[128,16,128]{2,1,0:T(8,128)S(1)}, u32[]{:S(2)}, u32[]{:S(2)}) async-start(f32[128,16,128]{2,1,0:T(8,128)} %stack.17), calls=%async_computation | async-start | bytes 2097152 | tf_op jit(solution)/shard_map/all_to_all | solution.py:122
  66.2 572.0 %all-reduce.10.cloned.1.call-start = ((), (), s32[]{:S(2)}) async-start(), calls=%async_computation.2 | async-start | bytes 262144 | tf_op jit(solution)/shard_map/psum | solution.py:36
  67.7 12.6 %copy-start.33 = (f32[12]{0:T(128)S(1)}, f32[12]{0:T(128)}, u32[]{:S(2)}) copy-start(f32[12]{0:T(128)} %param.22) | copy-start | bytes 148
  68.4 12.6 %collective-permute-start.6 = (f32[1,66,512]{2,1,0:T(8,128)}, f32[1,66,512]{2,1,0:T(8,128)S(1)}, u32[]{:S(2)}, u32[]{:S(2)}) collective-permute-start(f32[1,66,512]{2,1,0:T(8,128)} %get-tuple-element.179), channel_id=1, source_target_pairs={{0,1},{1,2},{2,3},{4,5},{5,6},{6,7},{8,9},{9,10},{10,11},{12,13},{... | collective-permute-start | bytes 405512 | tf_op jit(solution)/shard_map/ppermute | solution.py:26
  71.9 9.1 collective-permute-start.7
  74.4 9.9 %collective-permute-start.2 = (f32[2,1,66,512]{3,2,1,0:T(8,128)S(1)}, f32[2,1,66,512]{3,2,1,0:T(8,128)S(1)}, u32[]{:S(2)}, u32[]{:S(2)}) collective-permute-start(f32[2,1,66,512]{3,2,1,0:T(8,128)S(1)} %get-tuple-element.163), channel_id=1, source_target_pairs={{0,1},{1,2},{2,3},{4,5},{5,6},{6,7},{8,9},{9,10},{10,11},{12,13},{... | collective-permute-start | bytes 811016 | tf_op jit(solution)/shard_map/ppermute | solution.py:26
  77.9 9.6 collective-permute-start.3
  120.3 344.5 %copy-start.9 = (f32[2,64,512]{2,1,0:T(8,128)S(1)}, f32[2,64,512]{2,1,0:T(8,128)}, u32[]{:S(2)}) copy-start(f32[2,64,512]{2,1,0:T(8,128)} %get-tuple-element.139) | copy-start | bytes 786436
  464.8 16.0 %copy-start.12 = (f32[1,64,512]{2,1,0:T(8,128)}, f32[1,64,512]{2,1,0:T(8,128)S(1)}, u32[]{:S(2)}) copy-start(f32[1,64,512]{2,1,0:T(8,128)S(1)} %mul.274) | copy-start | bytes 393220
  464.9 15.9 %copy-start.7 = (f32[2,64,512]{2,1,0:T(8,128)S(1)}, f32[2,64,512]{2,1,0:T(8,128)}, u32[]{:S(2)}) copy-start(f32[2,64,512]{2,1,0:T(8,128)} %get-tuple-element.141) | copy-start | bytes 786436
  465.0 2.6 collective-permute-start.8
  466.3 3.5 collective-permute-start.9
  469.9 7.0 collective-permute-start.10
  473.4 7.1 collective-permute-start.11
  481.3 4.5 collective-permute-start.12
  484.5 4.7 collective-permute-start.13
  489.2 7.2 collective-permute-start.14
  492.4 7.5 collective-permute-start.15
  501.6 10.1 %collective-permute-start.20 = (f32[2,1,512]{2,1,0:T(1,128)S(1)}, f32[2,1,512]{2,1,0:T(1,128)S(1)}, u32[]{:S(2)}, u32[]{:S(2)}) collective-permute-start(f32[2,1,512]{2,1,0:T(1,128)S(1)} %get-tuple-element.185), channel_id=1, source_target_pairs={{0,4},{4,8},{8,12},{12,16},{16,20},{20,24},{24,28},{28,32},{32,36}... | collective-permute-start | bytes 12296 | tf_op jit(solution)/shard_map/ppermute | solution.py:26
  504.5 7.3 collective-permute-start.21
  505.8 6.0 collective-permute-start.16
  510.5 4.3 collective-permute-start.17
  514.9 16.7 %collective-permute-start.18 = (f32[2,1,66,512]{3,2,1,0:T(8,128)S(1)}, f32[2,1,66,512]{3,2,1,0:T(8,128)S(1)}, u32[]{:S(2)}, u32[]{:S(2)}) collective-permute-start(f32[2,1,66,512]{3,2,1,0:T(8,128)S(1)} %get-tuple-element.161), channel_id=1, source_target_pairs={{0,1},{1,2},{2,3},{4,5},{5,6},{6,7},{8,9},{9,10},{10,11},{12,13},{... | collective-permute-start | bytes 811016 | tf_op jit(solution)/shard_map/ppermute | solution.py:26
  516.8 14.8 %collective-permute-start.19 = (f32[2,1,66,512]{3,2,1,0:T(8,128)S(1)}, f32[2,1,66,512]{3,2,1,0:T(8,128)S(1)}, u32[]{:S(2)}, u32[]{:S(2)}) collective-permute-start(f32[2,1,66,512]{3,2,1,0:T(8,128)S(1)} %get-tuple-element.162), channel_id=1, source_target_pairs={{1,0},{2,1},{3,2},{5,4},{6,5},{7,6},{9,8},{10,9},{11,10},{13,12},{... | collective-permute-start | bytes 811016 | tf_op jit(solution)/shard_map/ppermute | solution.py:29
  520.8 8.6 collective-permute-start.22
  522.7 8.6 collective-permute-start.23
  535.0 3.5 collective-permute-start.24
  537.2 4.9 collective-permute-start.25
  542.1 7.2 collective-permute-start.26
  544.1 7.2 collective-permute-start.27
  552.0 4.5 collective-permute-start.28
  555.2 5.3 collective-permute-start.29
  561.2 7.4 collective-permute-start.30
  563.1 7.2 collective-permute-start.31
  571.0 67.2 %copy-start.18 = (f32[2,64,512]{2,1,0:T(8,128)}, f32[2,64,512]{2,1,0:T(8,128)S(1)}, u32[]{:S(2)}) copy-start(f32[2,64,512]{2,1,0:T(8,128)S(1)} %div.91) | copy-start | bytes 786436
  571.8 385.9 %reduce-scatter.2.cloned.1.call-start = ((), (), s32[]{:S(2)}) async-start(), calls=%async_computation.3 | async-start | bytes 1056768 | tf_op jit(solution)/shard_map/reduce_scatter | solution.py:175
  638.2 54.6 %copy-start.19 = (f32[1,256,128]{2,1,0:T(8,128)S(1)}, f32[1,256,128]{2,1,0:T(8,128)}, u32[]{:S(2)}) copy-start(f32[1,256,128]{2,1,0:T(8,128)} %param.27) | copy-start | bytes 393220
  638.2 54.6 %copy-start.20 = (f32[256,128]{1,0:T(8,128)S(1)}, f32[256,128]{1,0:T(8,128)}, u32[]{:S(2)}) copy-start(f32[256,128]{1,0:T(8,128)} %get-tuple-element.135) | copy-start | bytes 393220
  (24 other events, 51.2 us)
Sparse Core Ops, SparseCore 0:
  571.9 66.2 all-reduce.9
  695.5 262.1 reduce-scatter.1
